TPU v7x, 32 devices: a whole 2x2x4 slice. The times are simulated.
32 devices in a mesh: rows: 16 (over z, y, core), cent: 2 (over x).
Axes of the slice: x: 2, y: 2, z: 4, core: 2. Of those that a mesh axis runs over, the one named last changes fastest.
Arguments:
- vectors: bfloat16 [32768, 1024], P('rows'), may hold values from -40 to 40
- centroids: bfloat16 [1024, 4096], P('rows', 'cent'), may hold values from -8 to 8
Outputs:
- centroid_sums: float32 [1024, 4096], P('rows', 'cent')
All inputs are finite; a program needn't handle non-finite values.
Results may differ from a plain program's by a relative error of at most 0.0017.
Values may be sent and summed in bfloat16 or wider, within the bound.
A program may use at most 64 MiB of HBM per device.

v0:
```python
import functools
import math

import jax
import jax.numpy as jnp
from jax import lax
from jax.experimental import pallas as pl
from jax.experimental.pallas import tpu as pltpu
from jax.sharding import PartitionSpec as P

ITERS = 3
SHARPNESS = 3.0
MESH = pl.DeviceIdType.MESH
LANES = 128
SHARES = 2


def short_steps(ring):
    steps = 0
    while (steps + 1) * (steps + 2) / 2 <= 0.65 * ring:
        steps += 1
    return steps


def position_of(row, ring):
    chips = ring // 2
    chip, core = row // 2, row % 2
    far, near = chip // 2, chip % 2
    place = far + near * (chips - 1 - 2 * far)
    return place * 2 + core


def row_at(position, ring):
    chips = ring // 2
    place, core = position // 2, position % 2
    half = chips // 2
    near = place // half
    far = place + near * (chips - 1 - 2 * place)
    return (far * 2 + near) * 2 + core


def kernel(ring, groups, shorts, total_rows, columns_total, vec_ref, cen_ref, out_ref, cen_full, vec_t, bal, wts, rows_b,
           part, row_x, col_x, short_out, short_in, sum_in, ag_send, ag_recv, row_send, row_recv, col_send, col_recv, rs_send, rs_recv):
    rows, width = vec_ref.shape
    depth, cols = cen_ref.shape
    me = lax.axis_index("rows")
    my_group = lax.axis_index("cent")
    pos = position_of(me, ring)
    right = row_at((pos + 1) % ring, ring)
    left = row_at((pos + ring - 1) % ring, ring)
    neighbours = (right, left)
    chunks = min(4, cols // LANES)
    cw = cols // chunks

    barrier = pltpu.get_barrier_semaphore()

    def greet(o, carry):
        pl.semaphore_signal(barrier, inc=1, device_id={"rows": (me + o) % ring}, device_id_type=MESH)
        return carry

    lax.fori_loop(1, ring, greet, 0)
    for o in range(1, groups):
        pl.semaphore_signal(barrier, inc=1, device_id={"cent": (my_group + o) % groups}, device_id_type=MESH)

    tile = 256

    mine = pl.ds(pl.multiple_of(me * depth, depth), depth)
    cen_full[mine, :] = cen_ref[...]
    pl.semaphore_wait(barrier, ring - 1 + groups - 1)

    steps = (ring // 2, ring // 2 - 1)

    def gather_copy(way, step, chunk):
        source = (pos + ring - step) % ring if way == 0 else (pos + step) % ring
        block = row_at(source, ring)
        view = cen_full.at[pl.ds(pl.multiple_of(block * depth, depth), depth), pl.ds(chunk * cw, cw)]
        return pltpu.make_async_remote_copy(
            src_ref=view, dst_ref=view, send_sem=ag_send.at[way, step, chunk], recv_sem=ag_recv.at[way, step, chunk],
            device_id={"rows": neighbours[way]}, device_id_type=MESH)

    def gather_arrival(way, step, chunk):
        source = (pos + ring - step - 1) % ring if way == 0 else (pos + step + 1) % ring
        block = row_at(source, ring)
        view = cen_full.at[pl.ds(pl.multiple_of(block * depth, depth), depth), pl.ds(chunk * cw, cw)]
        return pltpu.make_async_remote_copy(
            src_ref=view, dst_ref=view, send_sem=ag_send.at[way, step, chunk], recv_sem=ag_recv.at[way, step, chunk],
            device_id={"rows": neighbours[way]}, device_id_type=MESH)

    for chunk in range(chunks):
        for way in range(2):
            gather_copy(way, 0, chunk).start()

    def turn(t, carry):
        at = pl.ds(pl.multiple_of(t * tile, tile), tile)
        vec_t[:, at] = vec_ref[at, :].T
        return carry

    lax.fori_loop(0, rows // tile, turn, 0)

    def gather_step(step, carry):
        for chunk in range(chunks):
            for way in range(2):
                gather_arrival(way, step - 1, chunk).wait_recv()
                gather_copy(way, step, chunk).start()
        return carry

    lax.fori_loop(1, steps[1], gather_step, 0)
    last = steps[1]
    for chunk in range(chunks):
        gather_arrival(0, last - 1, chunk).wait_recv()
        gather_copy(0, last, chunk).start()
        gather_arrival(1, last - 1, chunk).wait_recv()
    for chunk in range(chunks):
        gather_arrival(0, last, chunk).wait_recv()

    scale = SHARPNESS / math.sqrt(width)
    strips = cols // LANES

    share = rows // SHARES

    def rows_of(part_):
        return pl.ds(part_ * share, share)

    def to_lanes(op, part_):
        return op(part[rows_of(part_), :].T, axis=0, keepdims=True)

    def to_rows(vector, part_):
        rows_b[rows_of(part_), :] = jnp.broadcast_to(vector, (LANES, share)).T

    def score(t, carry):
        at = pl.ds(pl.multiple_of(t * tile, tile), tile)
        top = None
        for chunk in range(chunks):
            s = jnp.dot(vec_ref[at, :], cen_full[:, chunk * cw:(chunk + 1) * cw],
                        preferred_element_type=jnp.float32) * scale
            bal[at, chunk * cw:(chunk + 1) * cw] = s
            for j in range(cw // LANES):
                piece = s[:, j * LANES:(j + 1) * LANES]
                top = piece if top is None else jnp.maximum(top, piece)
        part[at, :] = jnp.broadcast_to(jnp.max(top, axis=1, keepdims=True), (tile, LANES))
        return carry

    lax.fori_loop(0, rows // tile, score, 0)
    small = 32
    per_share = share // small

    def exponent(t, carry):
        at = pl.ds(pl.multiple_of(t * small, small), small)
        m = part[at, :]
        acc = None
        for j in range(strips):
            lanes = slice(j * LANES, (j + 1) * LANES)
            e = jnp.exp(bal[at, lanes] - m)
            bal[at, lanes] = e
            acc = e if acc is None else acc + e
        part[at, :] = acc
        return carry

    def row_copy(turn_, part_, o):
        return pltpu.make_async_remote_copy(
            src_ref=row_x.at[turn_, part_, 0], dst_ref=row_x.at[turn_, part_, o],
            send_sem=row_send.at[turn_, part_, o], recv_sem=row_recv.at[turn_, part_, o],
            device_id={"cent": (my_group + o) % groups}, device_id_type=MESH)

    def col_copy(turn_, o):
        return pltpu.make_async_remote_copy(
            src_ref=col_x.at[turn_, 0], dst_ref=col_x.at[turn_, o], send_sem=col_send.at[turn_, o],
            recv_sem=col_recv.at[turn_, o], device_id={"rows": (me + o) % ring}, device_id_type=MESH)

    def send_rows(turn_, part_):
        for o in range(1, groups):
            row_copy(turn_, part_, o).start()

    def receive_rows(turn_, part_):
        for o in range(1, groups):
            row_copy(turn_, part_, o).wait_recv()

    for part_ in range(SHARES):
        row_x[0, part_, 0, 0:1, :] = to_lanes(jnp.max, part_)
        lax.fori_loop(part_ * per_share, (part_ + 1) * per_share, exponent, 0)
        row_x[0, part_, 0, 1:2, :] = to_lanes(jnp.sum, part_)
        send_rows(0, part_)

    def softmax_rows(part_):
        receive_rows(0, part_)
        tops = [row_x[0, part_, o, 0:1, :] for o in range(groups)]
        sums = [row_x[0, part_, o, 1:2, :] for o in range(groups)]
        highest = functools.reduce(jnp.maximum, tops)
        total = functools.reduce(jnp.add, [s * jnp.exp(m - highest) for s, m in zip(sums, tops)])
        to_rows(jnp.exp(tops[0] - highest) / total, part_)

    def balance_rows(turn_, part_):
        receive_rows(turn_, part_)
        mass = functools.reduce(jnp.add, [row_x[turn_, part_, o, 0:1, :] for o in range(groups)])
        to_rows(1.0 / mass, part_)

    target = total_rows / columns_total

    def column_pass(column_scale, part_, accs):
        def body(t, accs):
            at = pl.ds(pl.multiple_of(t * small, small), small)
            r = rows_b[at, :]
            new = []
            for j in range(strips):
                lanes = slice(j * LANES, (j + 1) * LANES)
                b = bal[at, lanes]
                if column_scale is not None:
                    b = b * column_scale[:, lanes]
                b = b * r
                bal[at, lanes] = b
                folded = accs[j]
                for q in range(small // 8):
                    folded = folded + b[q * 8:(q + 1) * 8, :]
                new.append(folded)
            return tuple(new)

        return lax.fori_loop(part_ * per_share, (part_ + 1) * per_share, body, accs)

    def row_pass(column_scale, part_):
        def body(t, carry):
            at = pl.ds(pl.multiple_of(t * small, small), small)
            acc = None
            for j in range(strips):
                lanes = slice(j * LANES, (j + 1) * LANES)
                b = bal[at, lanes] * column_scale[:, lanes]
                acc = b if acc is None else acc + b
            part[at, :] = acc
            return carry

        lax.fori_loop(part_ * per_share, (part_ + 1) * per_share, body, 0)
        return to_lanes(jnp.sum, part_)

    column_scale = None
    for it in range(ITERS):
        accs = tuple(jnp.zeros((8, LANES), jnp.float32) for _ in range(strips))
        for part_ in range(SHARES):
            if it == 0:
                softmax_rows(part_)
            else:
                balance_rows(it, part_)
            accs = column_pass(column_scale, part_, accs)
        for j in range(strips):
            col_x[it, 0, :, j * LANES:(j + 1) * LANES] = jnp.sum(accs[j], axis=0, keepdims=True)

        def send(o, carry, it=it):
            col_copy(it, o).start()
            return carry

        def receive(o, acc, it=it):
            col_copy(it, o).wait_recv()
            return acc + col_x[it, o]

        lax.fori_loop(1, ring, send, 0)
        mass = lax.fori_loop(1, ring, receive, col_x[it, 0])
        column_scale = target / mass
        for part_ in range(SHARES):
            row_x[it + 1, part_, 0, 0:1, :] = row_pass(column_scale, part_)
            send_rows(it + 1, part_)

    def weigh(t, carry):
        at = pl.ds(pl.multiple_of(t * small, small), small)
        r = rows_b[at, :]
        for j in range(strips):
            lanes = slice(j * LANES, (j + 1) * LANES)
            wts[at, lanes] = (bal[at, lanes] * column_scale[:, lanes] * r).astype(jnp.bfloat16)
        return carry

    for part_ in range(SHARES):
        balance_rows(ITERS, part_)
        lax.fori_loop(part_ * per_share, (part_ + 1) * per_share, weigh, 0)

    dt = min(256, width)
    factor = columns_total / total_rows

    def block_at(way, step):
        where = (pos + 2 * ring - 1 - step) % ring if way == 0 else (pos + 1 + step) % ring
        return pl.ds(pl.multiple_of(row_at(where, ring) * depth, depth), depth)

    pieces = chunks
    half = pieces // 2

    def sum_copy(piece, step):
        way = 0 if piece < half else 1
        lanes = pl.ds(piece * cw, cw)
        if step < shorts:
            source, target_ = short_out.at[step, piece], short_in.at[step, piece]
        else:
            source, target_ = bal.at[block_at(way, step), lanes], sum_in.at[step - shorts, piece]
        return pltpu.make_async_remote_copy(
            src_ref=source, dst_ref=target_, send_sem=rs_send.at[step, piece], recv_sem=rs_recv.at[step, piece],
            device_id={"rows": neighbours[way]}, device_id_type=MESH)

    def arrived(piece, step):
        if step < shorts:
            return short_in[step, piece].astype(jnp.float32)
        return sum_in[step - shorts, piece]

    def advance(piece, step):
        way = 0 if piece < half else 1
        lanes = slice(piece * cw, (piece + 1) * cw)
        at = mine if step == ring - 1 else block_at(way, step)
        value = bal[at, lanes]
        if step > 0:
            sum_copy(piece, step - 1).wait_recv()
            value = value + arrived(piece, step - 1)
        if step == ring - 1:
            out_ref[:, lanes] = value
            return
        if step < shorts:
            short_out[step, piece] = value.astype(jnp.bfloat16)
        elif step > 0:
            bal[at, lanes] = value
        sum_copy(piece, step).start()

    order = [p + w * half for p in range(half) for w in range(2)]
    done = {}
    tiles = width // dt
    for piece in order:
        lanes = slice(piece * cw, (piece + 1) * cw)

        def multiply(t, carry, lanes=lanes):
            at = pl.ds(pl.multiple_of(t * dt, dt), dt)
            bal[at, lanes] = jnp.dot(vec_t[at, :], wts[:, lanes], preferred_element_type=jnp.float32) * factor
            return carry

        lax.fori_loop(0, tiles, multiply, 0)
        advance(piece, 0)
        done[piece] = 1
    while min(done.values()) < ring:
        for piece in order:
            if done[piece] < ring:
                advance(piece, done[piece])
                done[piece] += 1

    def drain_gather(step, carry):
        for chunk in range(chunks):
            for way in range(2):
                gather_copy(way, step, chunk).wait_send()
        return carry

    lax.fori_loop(0, steps[1], drain_gather, 0)
    for chunk in range(chunks):
        gather_copy(0, steps[1], chunk).wait_send()
    for turn_ in range(ITERS + 1):
        for part_ in range(SHARES):
            for o in range(1, groups):
                row_copy(turn_, part_, o).wait_send()

    def drain_columns(o, carry):
        for it in range(ITERS):
            col_copy(it, o).wait_send()
        return carry

    lax.fori_loop(1, ring, drain_columns, 0)

    for step in range(ring - 1):
        for piece in order:
            sum_copy(piece, step).wait_send()


def solution(mesh):
    ring, groups = mesh.shape["rows"], mesh.shape["cent"]

    def on_device(vectors, centroids):
        rows, width = vectors.shape
        depth, cols = centroids.shape
        chunks = min(4, cols // LANES)
        shorts = short_steps(ring)
        f32, bf16 = jnp.float32, jnp.bfloat16
        dma = pltpu.SemaphoreType.DMA
        return pl.pallas_call(
            functools.partial(kernel, ring, groups, shorts, rows * ring, cols * groups),
            out_shape=jax.ShapeDtypeStruct((depth, cols), f32),
            in_specs=[pl.BlockSpec(memory_space=pltpu.VMEM)] * 2,
            out_specs=pl.BlockSpec(memory_space=pltpu.VMEM),
            scratch_shapes=[
                pltpu.VMEM((width, cols), bf16),
                pltpu.VMEM((width, rows), bf16),
                pltpu.VMEM((max(rows, width), cols), f32),
                pltpu.VMEM((rows, cols), bf16),
                pltpu.VMEM((rows, LANES), f32),
                pltpu.VMEM((rows, LANES), f32),
                pltpu.VMEM((ITERS + 1, SHARES, groups, 2, rows // SHARES), f32),
                pltpu.VMEM((ITERS, ring, 1, cols), f32),
                pltpu.VMEM((shorts, chunks, depth, cols // chunks), bf16),
                pltpu.VMEM((shorts, chunks, depth, cols // chunks), bf16),
                pltpu.VMEM((ring - 1 - shorts, chunks, depth, cols // chunks), f32),
                dma((2, ring // 2, chunks)),
                dma((2, ring // 2, chunks)),
                dma((ITERS + 1, SHARES, groups)),
                dma((ITERS + 1, SHARES, groups)),
                dma((ITERS, ring)),
                dma((ITERS, ring)),
                dma((ring - 1, chunks)),
                dma((ring - 1, chunks)),
            ],
            compiler_params=pltpu.CompilerParams(
                collective_id=0, has_side_effects=True, vmem_limit_bytes=66 * 1000 * 1000),
        )(vectors, centroids)

    return jax.shard_map(
        on_device,
        mesh=mesh,
        in_specs=(P("rows", None), P("rows", "cent")),
        out_specs=P("rows", "cent"),
        check_vma=False,
    )
```

profile of v0, /device:TPU:0, one launch (start us, length us, event | category | flops | bytes accessed | tf_op | source)
XLA Modules:
  0.0 142.4 jit_solution(8646943408000959196)
XLA Ops:
  0.0 140.5 %shard_map.28 = f32[64,2048]{1,0:T(8,128)} custom-call(bf16[2048,1024]{1,0:T(8,128)(2,1)} %vec_ref.1, bf16[64,2048]{1,0:T(8,128)(2,1)} %cen_ref.1), custom_call_target="tpu_custom_call" | custom-call | tf_op jit(solution)/shard_map/pallas_call | solution.py:371
  140.5 1.9 %copy.4 = f32[64,2048]{1,0:T(8,128)} copy(f32[64,2048]{1,0:T(8,128)} %shard_map.28) | data formatting | bytes 1048576
where the time goes:
time: 143 us; the launch traced here: 142 us
  Pallas kernels  141 us (99%)
  local copies, waits for them, and re-layouts  1.87 us (1%)
    pallas_call x1, Pallas kernels, on_device(): pl.pallas_call(functools.partial(kernel, ring, groups, shorts, rows * rin...  141 us

commit v1 on v0

v1 whole, which is shorter than its diff:
```python
import functools
import math

import jax
import jax.numpy as jnp
from jax import lax
from jax.experimental import pallas as pl
from jax.experimental.pallas import tpu as pltpu
from jax.sharding import PartitionSpec as P

ITERS = 3
SHARPNESS = 3.0
VECTOR_BOUND = 40.0
MESH = pl.DeviceIdType.MESH
LANES = 128
SHARES = 2
f32, bf16 = jnp.float32, jnp.bfloat16


def position_of(chip, chips):
    far, near = chip // 2, chip % 2
    return far + near * (chips - 1 - 2 * far)


def chip_at(place, chips):
    near = place // (chips // 2)
    far = place + near * (chips - 1 - 2 * place)
    return far * 2 + near


def plan(ring, rows, width, depth, cols):
    chips, half, block = ring // 2, cols // 2, 2 * depth
    chunk = min(256, half)
    spans = 2 if half >= 2 * chunk else 1
    return dict(
        chips=chips, half=half, block=block, chunk=chunk, spans=spans, chunks=half // chunk,
        pieces=half // spans // chunk, tile=min(1024, 2 * rows), steps=chips // 2,
        lots=max(1, half // 2 // LANES), wide=block % LANES == 0)


def encode(value):
    square = value * value
    return (square * (value * jnp.abs(value))).astype(bf16)


def decode(code):
    code = code.astype(f32)
    root = lax.rsqrt(lax.rsqrt(jnp.abs(code)))
    return jnp.where(code < 0, -root, root)


def kernel(ring, groups, total_rows, columns_total, vec_ref, cen_ref, out_ref, cen_full, vec_all, vec_t, bal, wts, acc, cen_t,
           top_s, sum_s, scale_s, row_acc, col_b, col_acc, row_x, col_x, rs_out, rs_in, last_in, own_in,
           ag_send, ag_recv, pair_send, pair_recv, vec_sem, row_send, row_recv, col_send, col_recv,
           rs_send, rs_recv, last_send, last_recv, own_sem):
    rows, width = vec_ref.shape
    depth, cols = cen_ref.shape
    p = plan(ring, rows, width, depth, cols)
    chips, half, block, chunk = p["chips"], p["half"], p["block"], p["chunk"]
    spans, pieces, tile, steps, lots = p["spans"], p["pieces"], p["tile"], p["steps"], p["lots"]
    chunks, wide = p["chunks"], p["wide"]
    both = 2 * rows
    strips = both // LANES
    per_share = strips // SHARES

    me = lax.axis_index("rows")
    cent = lax.axis_index("cent")
    chip, core = me // 2, me % 2
    other = 1 - core
    partner = chip * 2 + other
    pos = position_of(chip, chips)
    following = chip_at((pos + 1) % chips, chips)
    previous = chip_at((pos + chips - 1) % chips, chips)
    neighbours = (following, previous)

    def chip_behind(way, distance):
        where = (pos + 2 * chips - distance) % chips if way == 0 else (pos + distance) % chips
        return chip_at(where, chips)

    def remote(source, target, send, recv, device):
        return pltpu.make_async_remote_copy(
            src_ref=source, dst_ref=target, send_sem=send, recv_sem=recv, device_id=device, device_id_type=MESH)

    barrier = pltpu.get_barrier_semaphore()

    def greet(o, carry):
        pl.semaphore_signal(barrier, inc=1, device_id={"rows": (me + o) % ring}, device_id_type=MESH)
        return carry

    lax.fori_loop(1, ring, greet, 0)
    for o in range(1, groups):
        for row in (me, partner):
            pl.semaphore_signal(
                barrier, inc=1, device_id={"rows": row, "cent": (cent + o) % groups}, device_id_type=MESH)

    mine = pl.ds(pl.multiple_of(me * depth, depth), depth)
    my_rows = pl.ds(pl.multiple_of(core * rows, rows), rows)
    cen_full[mine, :] = cen_ref[:, pl.ds(pl.multiple_of(core * half, LANES), half)]
    vec_local = pltpu.make_async_copy(vec_ref, vec_all.at[my_rows, :], vec_sem.at[2])
    vec_local.start()
    pl.semaphore_wait(barrier, ring - 1 + 2 * (groups - 1))

    def piece_lanes(piece):
        return pl.ds(pl.multiple_of(piece * chunk, chunk), chunk)

    def own_copy(way, h, piece):
        view = cen_ref.at[:, pl.ds(pl.multiple_of(h * half + piece * chunk, LANES), chunk)]
        return remote(view, cen_full.at[mine, piece_lanes(piece)], ag_send.at[way, 0, h, piece],
                      ag_recv.at[way, 0, core, piece], {"rows": neighbours[way] * 2 + h})

    def pair_copy(piece):
        view = cen_ref.at[:, pl.ds(pl.multiple_of(other * half + piece * chunk, LANES), chunk)]
        return remote(view, cen_full.at[mine, piece_lanes(piece)], pair_send.at[piece], pair_recv.at[piece],
                      {"rows": partner})

    def gather_view(way, distance, sub, piece):
        start = (chip_behind(way, distance) * 2 + sub) * depth
        return cen_full.at[pl.ds(pl.multiple_of(start, depth), depth), piece_lanes(piece)]

    def gather_copy(way, step, sub, piece):
        view = gather_view(way, step, sub, piece)
        return remote(view, view, ag_send.at[way, step, sub, piece], ag_recv.at[way, step, sub, piece],
                      {"rows": neighbours[way] * 2 + core})

    def gather_arrival(way, step, sub, piece):
        view = gather_view(way, step + 1, sub, piece)
        return remote(view, view, ag_send.at[way, step, sub, piece], ag_recv.at[way, step, sub, piece],
                      {"rows": neighbours[way] * 2 + core})

    def forward(step, piece):
        for way in range(2):
            gather_arrival(way, step - 1, way, piece).wait_recv()
            gather_copy(way, step, way, piece).start()

        @pl.when(step < steps - 1)
        def _():
            for way in range(2):
                gather_arrival(way, step - 1, 1 - way, piece).wait_recv()
                gather_copy(way, step, 1 - way, piece).start()

    def forward_all(span, e):
        forward(1 + e // pieces, span * pieces + e % pieces)

    events = (steps - 1) * pieces

    def start_span(span):
        for q in range(pieces):
            piece = span * pieces + q
            for way in range(2):
                for h in range(2):
                    own_copy(way, h, piece).start()
            pair_copy(piece).start()

    def finish_span(span):
        for q in range(pieces):
            piece = span * pieces + q
            pair_copy(piece).wait_recv()
            for way in range(2):
                gather_arrival(way, steps - 2, 1 - way, piece).wait_recv()
                gather_arrival(way, steps - 1, way, piece).wait_recv()

    start_span(0)
    vec_copy = remote(vec_ref, vec_all.at[my_rows, :], vec_sem.at[0], vec_sem.at[1], {"rows": partner})
    vec_copy.start()

    turn_tile = 256

    def turn_rows(first):
        def turn(t, carry):
            at = pl.ds(pl.multiple_of(first + t * turn_tile, turn_tile), turn_tile)
            vec_t[:, at] = vec_all[at, :].T
            return carry

        lax.fori_loop(0, rows // turn_tile, turn, 0)

    vec_local.wait()
    turn_rows(core * rows)

    def forward_first(e, carry):
        forward_all(0, e)
        return carry

    lax.fori_loop(0, events, forward_first, 0)
    if spans > 1:
        start_span(1)
    vec_copy.wait_recv()
    turn_rows(other * rows)
    finish_span(0)

    scale = SHARPNESS / math.sqrt(width)
    tiles = both // tile
    units = chunks // spans * tiles

    def unit(u, carry):
        k, t = u // tiles, u % tiles
        columns = pl.ds(pl.multiple_of(k * chunk, chunk), chunk)
        at = pl.ds(pl.multiple_of(t * tile, tile), tile)

        @pl.when(t == 0)
        def _():
            cen_t[...] = cen_full[:, columns].T

        s = jnp.dot(cen_t[...], vec_t[:, at], preferred_element_type=f32) * scale
        top = s[0:8]
        for q in range(1, chunk // 8):
            top = jnp.maximum(top, s[q * 8:(q + 1) * 8])
        top = jnp.max(top, axis=0, keepdims=True)
        e = jnp.exp(s - top)
        total = e[0:8]
        for q in range(1, chunk // 8):
            total = total + e[q * 8:(q + 1) * 8]
        bal[columns, at] = e
        top_s[pl.ds(k, 1), at] = top
        sum_s[pl.ds(k, 1), at] = jnp.sum(total, axis=0, keepdims=True)
        return carry

    def unit_and_forward(u, carry):
        unit(u, carry)
        forward_all(1, u)
        return carry

    if spans > 1:
        shared = min(events, units)
        lax.fori_loop(0, shared, unit_and_forward, 0)
        lax.fori_loop(shared, units, unit, 0)

        def forward_rest(e, carry):
            forward_all(1, e)
            return carry

        lax.fori_loop(shared, events, forward_rest, 0)
        finish_span(1)
        lax.fori_loop(units, 2 * units, unit, 0)
    else:
        lax.fori_loop(0, units, unit, 0)

    partners = [(o, f) for o in range(groups) for f in range(2) if o + f > 0]

    def share_lanes(share):
        return slice(share * per_share * LANES, (share + 1) * per_share * LANES)

    def row_copy(turn_, share, o, f, both_rows):
        slot = o * 2 + f
        here = slice(0, 2) if both_rows else slice(0, 1)
        lanes = share_lanes(share)
        return remote(row_x.at[turn_, 0, here, lanes], row_x.at[turn_, slot, here, lanes],
                      row_send.at[turn_, share, slot], row_recv.at[turn_, share, slot],
                      {"rows": partner if f else me, "cent": (cent + o) % groups})

    def send_rows(turn_, share):
        for o, f in partners:
            row_copy(turn_, share, o, f, turn_ == 0).start()

    def receive_rows(turn_, share):
        for o, f in partners:
            row_copy(turn_, share, o, f, turn_ == 0).wait_recv()

    slots = [0] + [o * 2 + f for o, f in partners]

    for share in range(SHARES):
        lanes = share_lanes(share)
        tops = [top_s[k:k + 1, lanes] for k in range(chunks)]
        top = functools.reduce(jnp.maximum, tops)
        row_x[0, 0, 0:1, lanes] = top
        row_x[0, 0, 1:2, lanes] = functools.reduce(
            jnp.add, [sum_s[k:k + 1, lanes] * jnp.exp(tops[k] - top) for k in range(chunks)])
        send_rows(0, share)

    def softmax_rows(share):
        receive_rows(0, share)
        lanes = share_lanes(share)
        tops = [row_x[0, o, 0:1, lanes] for o in slots]
        top = functools.reduce(jnp.maximum, tops)
        total = functools.reduce(jnp.add, [row_x[0, o, 1:2, lanes] * jnp.exp(m - top) for o, m in zip(slots, tops)])
        for k in range(chunks):
            scale_s[k:k + 1, lanes] = jnp.exp(top_s[k:k + 1, lanes] - top) / total

    def balance_rows(turn_, share):
        receive_rows(turn_, share)
        lanes = share_lanes(share)
        scale_s[0:1, lanes] = 1.0 / functools.reduce(jnp.add, [row_x[turn_, o, 0:1, lanes] for o in slots])

    def strip(share, j):
        start = (share * per_share + j) * LANES
        return slice(start, start + LANES)

    def column_part(share, lot, scale_row):
        r = [jnp.broadcast_to(scale_s[scale_row:scale_row + 1, strip(share, j)], (8, LANES)) for j in range(per_share)]

        def body(t, carry):
            at = pl.ds(pl.multiple_of(lot * chunk + t * 8, 8), 8)
            sums = [None] * 4
            for j in range(per_share):
                b = bal[at, strip(share, j)] * r[j]
                sums[j % 4] = b if sums[j % 4] is None else sums[j % 4] + b
            total = (sums[0] + sums[1]) + (sums[2] + sums[3])
            col_acc[at, :] = total if share == 0 else col_acc[at, :] + total
            return carry

        lax.fori_loop(0, chunk // 8, body, 0, unroll=2)

    def row_part(share, lot, scaled_row):
        if scaled_row is not None:
            r = [jnp.broadcast_to(scale_s[scaled_row:scaled_row + 1, strip(share, j)], (8, LANES))
                 for j in range(per_share)]

        def body(t, sums):
            at = pl.ds(pl.multiple_of(lot * chunk + t * 8, 8), 8)
            c = col_b[at, :]
            new = []
            for j in range(per_share):
                b = bal[at, strip(share, j)]
                if scaled_row is not None:
                    b = b * r[j]
                b = b * c
                if scaled_row is not None:
                    bal[at, strip(share, j)] = b
                new.append(sums[j] + b)
            return tuple(new)

        if lot == 0:
            sums = tuple(jnp.zeros((8, LANES), f32) for _ in range(per_share))
        else:
            sums = tuple(row_acc[:, strip(share, j)] for j in range(per_share))
        sums = lax.fori_loop(0, chunk // 8, body, sums, unroll=2)
        for j in range(per_share):
            row_acc[:, strip(share, j)] = sums[j]

    def col_copy(it, lot, o):
        lanes = slice(lot * chunk, (lot + 1) * chunk)
        return remote(col_x.at[it, 0, :, lanes], col_x.at[it, o, :, lanes], col_send.at[it, lot, o],
                      col_recv.at[it, lot, o], {"rows": (chip + o) % chips * 2 + core})

    target = total_rows / columns_total

    def send_column(it, lot):
        lanes = slice(lot * chunk, (lot + 1) * chunk)
        col_x[it, 0, :, lanes] = jnp.sum(col_acc[lanes, :].T, axis=0, keepdims=True)

        def send(o, carry):
            col_copy(it, lot, o).start()
            return carry

        lax.fori_loop(1, chips, send, 0)

    def receive_column(it, lot, scale_before):
        lanes = slice(lot * chunk, (lot + 1) * chunk)

        def receive(o, carry):
            col_copy(it, lot, o).wait_recv()
            return carry + col_x[it, o, :, lanes]

        mass = lax.fori_loop(1, chips, receive, col_x[it, 0, :, lanes])
        c = target / mass
        col_b[lanes, :] = jnp.broadcast_to(c, (LANES, chunk)).T

    for it in range(ITERS):
        for share in range(SHARES):
            if it == 0:
                softmax_rows(share)
            else:
                balance_rows(it, share)
            for lot in range(chunks):
                column_part(share, lot, lot if it == 0 else 0)
                if share == SHARES - 1:
                    send_column(it, lot)
        for lot in range(chunks):
            receive_column(it, lot, None)
            for share in range(SHARES):
                row_part(share, lot, lot if it == 0 else None)
                if lot == chunks - 1:
                    lanes = share_lanes(share)
                    row_x[it + 1, 0, 0:1, lanes] = jnp.sum(row_acc[:, lanes], axis=0, keepdims=True)
                    send_rows(it + 1, share)

    def weigh(share):
        def body(t, carry):
            at = pl.ds(pl.multiple_of(t * 16, 16), 16)
            c = col_b[at, :]
            for j in range(per_share):
                wts[at, strip(share, j)] = (bal[at, strip(share, j)] * c * scale_s[0:1, strip(share, j)]).astype(bf16)
            return carry

        lax.fori_loop(0, half // 16, body, 0)

    for share in range(SHARES):
        balance_rows(ITERS, share)
        weigh(share)

    way_cols = half // 2
    limit = VECTOR_BOUND * columns_total
    lift = 2.0 ** math.floor(math.log2(3.0e9 / limit))
    factor = columns_total / total_rows * lift
    mt = min(256, way_cols)

    def block_rows(chip_):
        return pl.ds(pl.multiple_of(chip_ * block, block), block)

    def produce(j, carry):
        for way in range(2):
            pair = [chip_behind(way, 2 * j + 1), chip_behind(way, 2 * j + 2)]
            right = jnp.concatenate([vec_all[:, block_rows(q)] for q in pair], axis=1)
            for m in range(way_cols // mt):
                at = slice(way * way_cols + m * mt, way * way_cols + (m + 1) * mt)
                s = (jnp.dot(wts[at, :], right, preferred_element_type=f32) * factor).T
                for i, q in enumerate(pair):
                    acc[block_rows(q), at] = s[i * block:(i + 1) * block]
        return carry

    def produce_all():
        dt = min(256, width)

        def body(t, carry):
            at = pl.ds(pl.multiple_of(t * dt, dt), dt)
            for m in range(half // mt):
                lanes = slice(m * mt, (m + 1) * mt)
                acc[at, lanes] = (jnp.dot(wts[lanes, :], vec_all[:, at], preferred_element_type=f32) * factor).T
            return carry

        lax.fori_loop(0, width // dt, body, 0)

    lw = way_cols // lots if way_cols % LANES == 0 else way_cols

    def lot_lanes(way, lot):
        return slice(way * way_cols + lot * lw, way * way_cols + (lot + 1) * lw)

    lot_count = way_cols // lw

    def sum_copy(way, lot, step):
        lanes = lot_lanes(way, lot)
        return remote(rs_out.at[step, :, lanes], rs_in.at[step, :, lanes], rs_send.at[step, way, lot],
                      rs_recv.at[step, way, lot], {"rows": neighbours[way] * 2 + core})

    def last_copy(way, lot, a):
        lanes = lot_lanes(way, lot)
        return remote(rs_out.at[chips - 2, a * depth:(a + 1) * depth, lanes], last_in.at[core, :, lanes],
                      last_send.at[a, way, lot], last_recv.at[core, way, lot], {"rows": neighbours[way] * 2 + a})

    def last_arrival(way, lot, h):
        lanes = lot_lanes(way, lot)
        return remote(rs_out.at[chips - 2, 0:depth, lanes], last_in.at[h, :, lanes],
                      last_send.at[0, way, lot], last_recv.at[h, way, lot], {"rows": neighbours[way] * 2 + core})

    def sum_step(step, first=False, last=False):
        for lot in range(lot_count):
            for way in range(2):
                lanes = lot_lanes(way, lot)
                value = acc[block_rows(chip_behind(way, step + 1)), lanes]
                if not first:
                    sum_copy(way, lot, step - 1).wait_recv()
                    value = value + decode(rs_in[step - 1, :, lanes])
                rs_out[step, :, lanes] = encode(value)
                if last:
                    for a in range(2):
                        last_copy(way, lot, a).start()
                else:
                    sum_copy(way, lot, step).start()

    if wide:
        produce(0, 0)
    else:
        produce_all()
    sum_step(0, first=True)

    def double_step(j, carry):
        if wide:
            produce(j, 0)
        sum_step(2 * j - 1)
        sum_step(2 * j)
        return carry

    lax.fori_loop(1, chips // 2 - 1, double_step, 0)
    if wide:
        produce(chips // 2 - 1, 0)
    own_copy_sum = remote(acc.at[pl.ds(pl.multiple_of(partner * depth, depth), depth), :], own_in,
                          own_sem.at[0], own_sem.at[1], {"rows": partner})
    own_copy_sum.start()
    sum_step(chips - 3)
    sum_step(chips - 2, last=True)

    own_copy_sum.wait_recv()
    for lot in range(lot_count):
        for way in range(2):
            lanes = lot_lanes(way, lot)
            for h, extra in ((core, acc[mine, lanes]), (other, own_in[:, lanes])):
                last_arrival(way, lot, h).wait_recv()
                value = decode(last_in[h, :, lanes]) + extra
                start = h * half + lanes.start
                out_ref[:, pl.ds(pl.multiple_of(start, lw if lw < LANES else LANES), lw)] = value * (1.0 / lift)

    for piece in range(spans * pieces):
        pair_copy(piece).wait_send()
        for way in range(2):
            for h in range(2):
                own_copy(way, h, piece).wait_send()

    def drain_gather(step, carry):
        for piece in range(spans * pieces):
            for way in range(2):
                gather_copy(way, step, way, piece).wait_send()

                @pl.when(step < steps - 1)
                def _():
                    gather_copy(way, step, 1 - way, piece).wait_send()
        return carry

    lax.fori_loop(1, steps, drain_gather, 0)
    vec_copy.wait_send()
    for turn_ in range(ITERS + 1):
        for share in range(SHARES):
            for o, f in partners:
                row_copy(turn_, share, o, f, turn_ == 0).wait_send()

    def drain_columns(o, carry):
        for it in range(ITERS):
            for lot in range(chunks):
                col_copy(it, lot, o).wait_send()
        return carry

    lax.fori_loop(1, chips, drain_columns, 0)

    def drain_sums(step, carry):
        for lot in range(lot_count):
            for way in range(2):
                sum_copy(way, lot, step).wait_send()
        return carry

    lax.fori_loop(0, chips - 2, drain_sums, 0)
    for lot in range(lot_count):
        for way in range(2):
            for a in range(2):
                last_copy(way, lot, a).wait_send()
    own_copy_sum.wait_send()


def solution(mesh):
    ring, groups = mesh.shape["rows"], mesh.shape["cent"]

    def on_device(vectors, centroids):
        rows, width = vectors.shape
        depth, cols = centroids.shape
        p = plan(ring, rows, width, depth, cols)
        chips, half, block, lots = p["chips"], p["half"], p["block"], p["lots"]
        both = 2 * rows
        pieces = p["spans"] * p["pieces"]
        dma = pltpu.SemaphoreType.DMA
        vmem = pltpu.VMEM
        return pl.pallas_call(
            functools.partial(kernel, ring, groups, rows * ring, cols * groups),
            out_shape=jax.ShapeDtypeStruct((depth, cols), f32),
            in_specs=[pl.BlockSpec(memory_space=pltpu.VMEM)] * 2,
            out_specs=pl.BlockSpec(memory_space=pltpu.VMEM),
            scratch_shapes=[
                vmem((width, half), bf16),
                vmem((both, width), bf16),
                vmem((width, both), bf16),
                vmem((half, both), f32),
                vmem((half, both), bf16),
                vmem((width, half), f32),
                vmem((p["chunk"], width), bf16),
                vmem((max(8, p["chunks"]), both), f32),
                vmem((max(8, p["chunks"]), both), f32),
                vmem((max(8, p["chunks"]), both), f32),
                vmem((8, both), f32),
                vmem((half, LANES), f32),
                vmem((half, LANES), f32),
                vmem((ITERS + 1, 2 * groups, 2, both), f32),
                vmem((ITERS, chips, 1, half), f32),
                vmem((chips - 1, block, half), bf16),
                vmem((chips - 2, block, half), bf16),
                vmem((2, depth, half), bf16),
                vmem((depth, half), f32),
                dma((2, p["steps"], 2, pieces)),
                dma((2, p["steps"], 2, pieces)),
                dma((pieces,)),
                dma((pieces,)),
                dma((3,)),
                dma((ITERS + 1, SHARES, 2 * groups)),
                dma((ITERS + 1, SHARES, 2 * groups)),
                dma((ITERS, p["chunks"], chips)),
                dma((ITERS, p["chunks"], chips)),
                dma((chips - 2, 2, lots)),
                dma((chips - 2, 2, lots)),
                dma((2, 2, lots)),
                dma((2, 2, lots)),
                dma((2,)),
            ],
            compiler_params=pltpu.CompilerParams(
                collective_id=0, has_side_effects=True, vmem_limit_bytes=66 * 1000 * 1000),
        )(vectors, centroids)

    return jax.shard_map(
        on_device,
        mesh=mesh,
        in_specs=(P("rows", None), P("rows", "cent")),
        out_specs=P("rows", "cent"),
        check_vma=False,
    )
```

time: 143 us -> 116 us (0.81)
  Pallas kernels: 141 us -> 114 us
    pallas_call x1, Pallas kernels: 141 us -> 114 us  [on_device(): pl.pallas_call(functools.partial(kernel, ring, groups, rows * ring, cols...]
where the time goes in v1:
time: 116 us
  Pallas kernels  114 us (98%)
  local copies, waits for them, and re-layouts  1.87 us (2%)
    pallas_call x1, Pallas kernels, on_device(): pl.pallas_call(functools.partial(kernel, ring, groups, rows * ring, cols...  114 us

profile of v1, /device:TPU:0, one launch (start us, length us, event | category | flops | bytes accessed | tf_op | source)
XLA Modules:
  0.0 116.2 jit_solution(14349413639017283181)
XLA Ops:
  0.0 114.3 %shard_map.28 = f32[64,2048]{1,0:T(8,128)} custom-call(bf16[2048,1024]{1,0:T(8,128)(2,1)} %vec_ref.1, bf16[64,2048]{1,0:T(8,128)(2,1)} %cen_ref.1), custom_call_target="tpu_custom_call" | custom-call | tf_op jit(solution)/shard_map/pallas_call | solution.py:548
  114.3 1.9 %copy.4 = f32[64,2048]{1,0:T(8,128)} copy(f32[64,2048]{1,0:T(8,128)} %shard_map.28) | data formatting | bytes 1048576

commit v2 on v1

v2 whole, which is shorter than its diff:
```python
import functools
import math

import jax
import jax.numpy as jnp
from jax import lax
from jax.experimental import pallas as pl
from jax.experimental.pallas import tpu as pltpu
from jax.sharding import PartitionSpec as P

ITERS = 3
SHARPNESS = 3.0
VECTOR_BOUND = 40.0
MESH = pl.DeviceIdType.MESH
LANES = 128
SHARES = 2
f32, bf16 = jnp.float32, jnp.bfloat16


def position_of(chip, chips):
    far, near = chip // 2, chip % 2
    return far + near * (chips - 1 - 2 * far)


def chip_at(place, chips):
    near = place // (chips // 2)
    far = place + near * (chips - 1 - 2 * place)
    return far * 2 + near


def plan(ring, rows, width, depth, cols):
    chips, half, block = ring // 2, cols // 2, 2 * depth
    chunk = min(256, half)
    return dict(
        chips=chips, half=half, block=block, chunk=chunk, chunks=half // chunk, tile=min(1024, 2 * rows),
        steps=chips // 2, lots=max(1, half // 2 // (2 * LANES)), wide=block % LANES == 0 and chips == 8)


def encode(value):
    square = value * value
    return (square * (value * jnp.abs(value))).astype(bf16)


def decode(code):
    code = code.astype(f32)
    root = lax.rsqrt(lax.rsqrt(jnp.abs(code)))
    return jnp.where(code < 0, -root, root)


def kernel(ring, groups, total_rows, columns_total, vec_hbm, cen_hbm, out_ref, cen_own, cen_full, vec_all, vec_t, bal, wts, acc, cen_t,
           top_s, sum_s, scale_s, row_acc, col_b, col_acc, row_x, col_x, rs_out, rs_in, last_in, own_in,
           ag_send, ag_recv, pair_sem, vec_sem, row_send, row_recv, col_send, col_recv,
           rs_send, rs_recv, last_send, last_recv, own_sem):
    rows, width = vec_hbm.shape
    depth, cols = cen_hbm.shape
    p = plan(ring, rows, width, depth, cols)
    chips, half, block, chunk = p["chips"], p["half"], p["block"], p["chunk"]
    tile, steps, lots = p["tile"], p["steps"], p["lots"]
    chunks, wide = p["chunks"], p["wide"]
    both = 2 * rows
    strips = both // LANES
    per_share = strips // SHARES

    me = lax.axis_index("rows")
    cent = lax.axis_index("cent")
    chip, core = me // 2, me % 2
    other = 1 - core
    partner = chip * 2 + other
    pos = position_of(chip, chips)
    following = chip_at((pos + 1) % chips, chips)
    previous = chip_at((pos + chips - 1) % chips, chips)
    neighbours = (following, previous)

    def chip_behind(way, distance):
        where = (pos + 2 * chips - distance) % chips if way == 0 else (pos + distance) % chips
        return chip_at(where, chips)

    def remote(source, target, send, recv, device):
        return pltpu.make_async_remote_copy(
            src_ref=source, dst_ref=target, send_sem=send, recv_sem=recv, device_id=device, device_id_type=MESH)

    mine = pl.ds(pl.multiple_of(me * depth, depth), depth)
    my_rows = pl.ds(pl.multiple_of(core * rows, rows), rows)
    cen_local = pltpu.make_async_copy(cen_hbm, cen_own, vec_sem.at[3])
    cen_local.start()
    vec_local = pltpu.make_async_copy(vec_hbm, vec_all.at[my_rows, :], vec_sem.at[2])
    vec_local.start()

    barrier = pltpu.get_barrier_semaphore()

    def greet(o, carry):
        pl.semaphore_signal(barrier, inc=1, device_id={"rows": (me + o) % ring}, device_id_type=MESH)
        return carry

    lax.fori_loop(1, ring, greet, 0)
    for o in range(1, groups):
        for row in (me, partner):
            pl.semaphore_signal(
                barrier, inc=1, device_id={"rows": row, "cent": (cent + o) % groups}, device_id_type=MESH)

    cen_local.wait()
    cen_full[mine, :] = cen_own[:, pl.ds(pl.multiple_of(core * half, LANES), half)]
    pl.semaphore_wait(barrier, ring - 1 + 2 * (groups - 1))

    def half_view(h):
        return cen_own.at[:, pl.ds(pl.multiple_of(h * half, LANES), half)]

    def own_copy(way, h):
        return remote(half_view(h), cen_full.at[mine, :], ag_send.at[way, 0, h],
                      ag_recv.at[way, 0, core], {"rows": neighbours[way] * 2 + h})

    pair_copy = remote(half_view(other), cen_full.at[mine, :], pair_sem.at[0], pair_sem.at[1], {"rows": partner})

    def gather_view(way, distance, sub):
        start = (chip_behind(way, distance) * 2 + sub) * depth
        return cen_full.at[pl.ds(pl.multiple_of(start, depth), depth), :]

    def gather_copy(way, step, sub):
        view = gather_view(way, step, sub)
        return remote(view, view, ag_send.at[way, step, sub], ag_recv.at[way, step, sub],
                      {"rows": neighbours[way] * 2 + core})

    def gather_arrival(way, step, sub):
        view = gather_view(way, step + 1, sub)
        return remote(view, view, ag_send.at[way, step, sub], ag_recv.at[way, step, sub],
                      {"rows": neighbours[way] * 2 + core})

    def forward(step, carry):
        for turn_ in range(2):
            for way in range(2):
                sub = way if turn_ == 0 else 1 - way
                gather_arrival(way, step - 1, sub).wait_recv()
                gather_copy(way, step, sub).start()
        return carry

    def forward_last():
        for way in range(2):
            gather_arrival(way, steps - 2, way).wait_recv()
            gather_copy(way, steps - 1, way).start()

    for h in range(2):
        for way in range(2):
            own_copy(way, h).start()
    pair_copy.start()
    vec_local.wait()
    vec_copy = remote(vec_all.at[my_rows, :], vec_all.at[my_rows, :], vec_sem.at[0], vec_sem.at[1], {"rows": partner})
    vec_copy.start()

    turn_tile = 256

    def turn_rows(first):
        def turn(t, carry):
            at = pl.ds(pl.multiple_of(first + t * turn_tile, turn_tile), turn_tile)
            vec_t[:, at] = vec_all[at, :].T
            return carry

        lax.fori_loop(0, rows // turn_tile, turn, 0)

    turn_rows(core * rows)

    scale = SHARPNESS / math.sqrt(width)

    def block_rows(chip_):
        return pl.ds(pl.multiple_of(chip_ * block, block), block)

    def score_pass(blocks, first, final, begin=0, end=chunks):
        tile_here = tile if final else min(2 * tile, both)
        depth_here = width if blocks is None else len(blocks) * block

        def per_chunk(k, carry):
            columns = pl.ds(pl.multiple_of(k * chunk, chunk), chunk)
            if blocks is None:
                cen_t[...] = cen_full[:, columns].T
            else:
                cen_t[:, 0:depth_here] = jnp.concatenate([cen_full[block_rows(q), columns] for q in blocks], axis=0).T

            def per_tile(t, carry):
                at = pl.ds(pl.multiple_of(t * tile_here, tile_here), tile_here)
                if blocks is None:
                    right = vec_t[:, at]
                else:
                    right = jnp.concatenate([vec_t[block_rows(q), at] for q in blocks], axis=0)
                s = jnp.dot(cen_t[:, 0:depth_here], right, preferred_element_type=f32)
                if not first:
                    s = bal[columns, at] + s
                if not final:
                    bal[columns, at] = s
                    return carry
                s = s * scale
                top = s[0:8]
                for q in range(1, chunk // 8):
                    top = jnp.maximum(top, s[q * 8:(q + 1) * 8])
                top = jnp.max(top, axis=0, keepdims=True)
                e = jnp.exp(s - top)
                total = e[0:8]
                for q in range(1, chunk // 8):
                    total = total + e[q * 8:(q + 1) * 8]
                bal[columns, at] = e
                top_s[pl.ds(k, 1), at] = top
                sum_s[pl.ds(k, 1), at] = jnp.sum(total, axis=0, keepdims=True)
                return carry

            return lax.fori_loop(0, both // tile_here, per_tile, carry)

        lax.fori_loop(begin, end, per_chunk, 0)

    def wait_last():
        for way in range(2):
            gather_arrival(way, steps - 1, way).wait_recv()

    lax.fori_loop(1, steps - 1, forward, 0)
    pair_copy.wait_recv()
    vec_copy.wait_recv()
    turn_rows(other * rows)
    if wide:
        near = [chip, chip_behind(0, 1), chip_behind(1, 1), chip_behind(0, 2)]
        score_pass(near, True, False, 0, chunks // 2)
        forward_last()
        score_pass(near, True, False, chunks // 2, chunks)
        for way in range(2):
            gather_arrival(way, steps - 2, 1 - way).wait_recv()
        wait_last()
        score_pass([chip_behind(1, 2), chip_behind(0, 3), chip_behind(1, 3), chip_behind(0, 4)], False, True)
    else:
        forward_last()
        for way in range(2):
            gather_arrival(way, steps - 2, 1 - way).wait_recv()
        wait_last()
        score_pass(None, True, True)

    partners = [(o, f) for o in range(groups) for f in range(2) if o + f > 0]

    def share_lanes(share):
        return slice(share * per_share * LANES, (share + 1) * per_share * LANES)

    def row_copy(turn_, share, o, f, both_rows):
        slot = o * 2 + f
        here = slice(0, 2) if both_rows else slice(0, 1)
        lanes = share_lanes(share)
        return remote(row_x.at[turn_, 0, here, lanes], row_x.at[turn_, slot, here, lanes],
                      row_send.at[turn_, share, slot], row_recv.at[turn_, share, slot],
                      {"rows": partner if f else me, "cent": (cent + o) % groups})

    def send_rows(turn_, share):
        for o, f in partners:
            row_copy(turn_, share, o, f, turn_ == 0).start()

    def receive_rows(turn_, share):
        for o, f in partners:
            row_copy(turn_, share, o, f, turn_ == 0).wait_recv()

    slots = [0] + [o * 2 + f for o, f in partners]

    for share in range(SHARES):
        lanes = share_lanes(share)
        tops = [top_s[k:k + 1, lanes] for k in range(chunks)]
        top = functools.reduce(jnp.maximum, tops)
        row_x[0, 0, 0:1, lanes] = top
        row_x[0, 0, 1:2, lanes] = functools.reduce(
            jnp.add, [sum_s[k:k + 1, lanes] * jnp.exp(tops[k] - top) for k in range(chunks)])
        send_rows(0, share)

    def softmax_rows(share):
        receive_rows(0, share)
        lanes = share_lanes(share)
        tops = [row_x[0, o, 0:1, lanes] for o in slots]
        top = functools.reduce(jnp.maximum, tops)
        total = functools.reduce(jnp.add, [row_x[0, o, 1:2, lanes] * jnp.exp(m - top) for o, m in zip(slots, tops)])
        for k in range(chunks):
            scale_s[k:k + 1, lanes] = jnp.exp(top_s[k:k + 1, lanes] - top) / total

    def balance_rows(turn_, share):
        receive_rows(turn_, share)
        lanes = share_lanes(share)
        scale_s[0:1, lanes] = 1.0 / functools.reduce(jnp.add, [row_x[turn_, o, 0:1, lanes] for o in slots])

    def strip(share, j):
        start = (share * per_share + j) * LANES
        return slice(start, start + LANES)

    def column_part(share, lot, scale_row):
        r = [jnp.broadcast_to(scale_s[scale_row:scale_row + 1, strip(share, j)], (8, LANES)) for j in range(per_share)]

        def body(t, carry):
            at = pl.ds(pl.multiple_of(lot * chunk + t * 8, 8), 8)
            sums = [None] * 4
            for j in range(per_share):
                b = bal[at, strip(share, j)] * r[j]
                sums[j % 4] = b if sums[j % 4] is None else sums[j % 4] + b
            total = (sums[0] + sums[1]) + (sums[2] + sums[3])
            col_acc[at, :] = total if share == 0 else col_acc[at, :] + total
            return carry

        lax.fori_loop(0, chunk // 8, body, 0, unroll=4)

    def row_part(share, scaled):
        sums = tuple(jnp.zeros((8, LANES), f32) for _ in range(per_share))

        def span(first, count, scale_row, sums):
            if scaled:
                r = [jnp.broadcast_to(scale_s[scale_row:scale_row + 1, strip(share, j)], (8, LANES))
                     for j in range(per_share)]

            def body(t, sums):
                at = pl.ds(pl.multiple_of(first + t * 8, 8), 8)
                c = col_b[at, :]
                new = []
                for j in range(per_share):
                    b = bal[at, strip(share, j)]
                    if scaled:
                        b = b * r[j]
                    b = b * c
                    if scaled:
                        bal[at, strip(share, j)] = b
                    new.append(sums[j] + b)
                return tuple(new)

            return lax.fori_loop(0, count, body, sums, unroll=4)

        if scaled:
            for k in range(chunks):
                sums = span(k * chunk, chunk // 8, k, sums)
        else:
            sums = span(0, half // 8, 0, sums)
        for j in range(per_share):
            row_acc[:, strip(share, j)] = sums[j]

    def col_copy(it, o):
        return remote(col_x.at[it, 0], col_x.at[it, o], col_send.at[it, o], col_recv.at[it, o],
                      {"rows": (chip + o) % chips * 2 + core})

    target = total_rows / columns_total

    def send_column(it):
        col_x[it, 0] = jnp.sum(col_acc[...].T, axis=0, keepdims=True)

        def send(o, carry):
            col_copy(it, o).start()
            return carry

        lax.fori_loop(1, chips, send, 0)

    def receive_column(it):
        def receive(o, carry):
            col_copy(it, o).wait_recv()
            return carry + col_x[it, o]

        mass = lax.fori_loop(1, chips, receive, col_x[it, 0])
        col_b[...] = jnp.broadcast_to(target / mass, (LANES, half)).T

    for it in range(ITERS):
        for share in range(SHARES):
            if it == 0:
                softmax_rows(share)
            else:
                balance_rows(it, share)
            for lot in range(chunks):
                column_part(share, lot, lot if it == 0 else 0)
        send_column(it)
        receive_column(it)
        for share in range(SHARES):
            row_part(share, it == 0)
            lanes = share_lanes(share)
            row_x[it + 1, 0, 0:1, lanes] = jnp.sum(row_acc[:, lanes], axis=0, keepdims=True)
            send_rows(it + 1, share)

    def weigh(first, count):
        for share in range(SHARES):
            def body(t, carry):
                at = pl.ds(pl.multiple_of(first + t * 16, 16), 16)
                c = col_b[at, :]
                for j in range(per_share):
                    r = scale_s[0:1, strip(share, j)]
                    wts[at, strip(share, j)] = (bal[at, strip(share, j)] * c * r).astype(bf16)
                return carry

            lax.fori_loop(0, count // 16, body, 0)

    for share in range(SHARES):
        balance_rows(ITERS, share)

    way_cols = half // 2
    limit = VECTOR_BOUND * columns_total
    lift = 2.0 ** math.floor(math.log2(3.0e9 / limit))
    factor = columns_total / total_rows * lift
    lw = way_cols // lots

    def produce(way, lot, j):
        pair = [chip_behind(way, 2 * j + 1), chip_behind(way, 2 * j + 2)]
        right = jnp.concatenate([vec_all[:, block_rows(q)] for q in pair], axis=1)
        at = lot_lanes(way, lot)
        s = (jnp.dot(wts[at, :], right, preferred_element_type=f32) * factor).T
        for i, q in enumerate(pair):
            acc[block_rows(q), at] = s[i * block:(i + 1) * block]

    def produce_all():
        dt, mt = min(256, width), min(256, way_cols)

        def body(t, carry):
            at = pl.ds(pl.multiple_of(t * dt, dt), dt)
            for m in range(half // mt):
                lanes = slice(m * mt, (m + 1) * mt)
                acc[at, lanes] = (jnp.dot(wts[lanes, :], vec_all[:, at], preferred_element_type=f32) * factor).T
            return carry

        lax.fori_loop(0, width // dt, body, 0)

    def lot_lanes(way, lot):
        return slice(way * way_cols + lot * lw, way * way_cols + (lot + 1) * lw)

    lot_count = lots

    def sum_copy(way, lot, step):
        lanes = lot_lanes(way, lot)
        return remote(rs_out.at[step, :, lanes], rs_in.at[step, :, lanes], rs_send.at[step, way, lot],
                      rs_recv.at[step, way, lot], {"rows": neighbours[way] * 2 + core})

    def last_copy(way, lot, a):
        lanes = lot_lanes(way, lot)
        return remote(rs_out.at[chips - 2, a * depth:(a + 1) * depth, lanes], last_in.at[core, :, lanes],
                      last_send.at[a, way, lot], last_recv.at[core, way, lot], {"rows": neighbours[way] * 2 + a})

    def last_arrival(way, lot, h):
        lanes = lot_lanes(way, lot)
        return remote(rs_out.at[chips - 2, 0:depth, lanes], last_in.at[h, :, lanes],
                      last_send.at[0, way, lot], last_recv.at[h, way, lot], {"rows": neighbours[way] * 2 + core})

    def sum_step(step, first=False, last=False, before=None, after=None):
        for lot in range(lot_count):
            values = []
            for way in range(2):
                if before is not None:
                    before(way, lot)
                if not first:
                    sum_copy(way, lot, step - 1).wait_recv()
            for way in range(2):
                lanes = lot_lanes(way, lot)
                value = acc[block_rows(chip_behind(way, step + 1)), lanes]
                if not first:
                    value = value + decode(rs_in[step - 1, :, lanes])
                values.append(encode(value))
            for way in range(2):
                rs_out[step, :, lot_lanes(way, lot)] = values[way]
            for way in range(2):
                if last:
                    for a in range(2):
                        last_copy(way, lot, a).start()
                else:
                    sum_copy(way, lot, step).start()
            if after is not None:
                after(lot)

    if wide:
        def first_produce(way, lot):
            weigh(way * way_cols + lot * lw, lw)
            produce(way, lot, 0)

        sum_step(0, first=True, before=first_produce)
        for lot in range(lot_count):
            produce(0, lot, 1)
        sum_step(1, after=lambda lot: produce(1, lot, 1))

        def double_step(j, carry):
            sum_step(2 * j, after=lambda lot: produce(0, lot, j + 1))
            sum_step(2 * j + 1, after=lambda lot: produce(1, lot, j + 1))
            return carry

        lax.fori_loop(1, chips // 2 - 1, double_step, 0)
    else:
        weigh(0, half)
        produce_all()
        sum_step(0, first=True)

        def single_step(step, carry):
            sum_step(step)
            return carry

        lax.fori_loop(1, chips - 2, single_step, 0)
    own_copy_sum = remote(acc.at[pl.ds(pl.multiple_of(partner * depth, depth), depth), :], own_in,
                          own_sem.at[0], own_sem.at[1], {"rows": partner})
    own_copy_sum.start()
    sum_step(chips - 2, last=True)

    own_copy_sum.wait_recv()
    for lot in range(lot_count):
        for way in range(2):
            lanes = lot_lanes(way, lot)
            for h, extra in ((core, acc[mine, lanes]), (other, own_in[:, lanes])):
                last_arrival(way, lot, h).wait_recv()
                value = decode(last_in[h, :, lanes]) + extra
                start = h * half + lanes.start
                out_ref[:, pl.ds(pl.multiple_of(start, lw if lw < LANES else LANES), lw)] = value * (1.0 / lift)

    pair_copy.wait_send()
    for way in range(2):
        for h in range(2):
            own_copy(way, h).wait_send()

    def drain_gather(step, carry):
        for way in range(2):
            for sub in range(2):
                gather_copy(way, step, sub).wait_send()
        return carry

    lax.fori_loop(1, steps - 1, drain_gather, 0)
    for way in range(2):
        gather_copy(way, steps - 1, way).wait_send()
    vec_copy.wait_send()
    for turn_ in range(ITERS + 1):
        for share in range(SHARES):
            for o, f in partners:
                row_copy(turn_, share, o, f, turn_ == 0).wait_send()

    def drain_columns(o, carry):
        for it in range(ITERS):
            col_copy(it, o).wait_send()
        return carry

    lax.fori_loop(1, chips, drain_columns, 0)

    def drain_sums(step, carry):
        for lot in range(lot_count):
            for way in range(2):
                sum_copy(way, lot, step).wait_send()
        return carry

    lax.fori_loop(0, chips - 2, drain_sums, 0)
    for lot in range(lot_count):
        for way in range(2):
            for a in range(2):
                last_copy(way, lot, a).wait_send()
    own_copy_sum.wait_send()


def solution(mesh):
    ring, groups = mesh.shape["rows"], mesh.shape["cent"]

    def on_device(vectors, centroids):
        rows, width = vectors.shape
        depth, cols = centroids.shape
        p = plan(ring, rows, width, depth, cols)
        chips, half, block, lots = p["chips"], p["half"], p["block"], p["lots"]
        both = 2 * rows
        dma = pltpu.SemaphoreType.DMA
        vmem = pltpu.VMEM
        return pl.pallas_call(
            functools.partial(kernel, ring, groups, rows * ring, cols * groups),
            out_shape=jax.ShapeDtypeStruct((depth, cols), f32),
            in_specs=[pl.BlockSpec(memory_space=pl.ANY)] * 2,
            out_specs=pl.BlockSpec(memory_space=pltpu.VMEM),
            scratch_shapes=[
                vmem((depth, cols), bf16),
                vmem((width, half), bf16),
                vmem((both, width), bf16),
                vmem((width, both), bf16),
                vmem((half, both), f32),
                vmem((half, both), bf16),
                vmem((width, half), f32),
                vmem((p["chunk"], width), bf16),
                vmem((max(8, p["chunks"]), both), f32),
                vmem((max(8, p["chunks"]), both), f32),
                vmem((max(8, p["chunks"]), both), f32),
                vmem((8, both), f32),
                vmem((half, LANES), f32),
                vmem((half, LANES), f32),
                vmem((ITERS + 1, 2 * groups, 2, both), f32),
                vmem((ITERS, chips, 1, half), f32),
                vmem((chips - 1, block, half), bf16),
                vmem((chips - 2, block, half), bf16),
                vmem((2, depth, half), bf16),
                vmem((depth, half), f32),
                dma((2, p["steps"], 2)),
                dma((2, p["steps"], 2)),
                dma((2,)),
                dma((4,)),
                dma((ITERS + 1, SHARES, 2 * groups)),
                dma((ITERS + 1, SHARES, 2 * groups)),
                dma((ITERS, chips)),
                dma((ITERS, chips)),
                dma((chips - 2, 2, lots)),
                dma((chips - 2, 2, lots)),
                dma((2, 2, lots)),
                dma((2, 2, lots)),
                dma((2,)),
            ],
            compiler_params=pltpu.CompilerParams(
                collective_id=0, has_side_effects=True, vmem_limit_bytes=66 * 1000 * 1000),
        )(vectors, centroids)

    return jax.shard_map(
        on_device,
        mesh=mesh,
        in_specs=(P("rows", None), P("rows", "cent")),
        out_specs=P("rows", "cent"),
        check_vma=False,
    )
```

time: 116 us -> 110 us (0.948)
  Pallas kernels: 114 us -> 108 us
    pallas_call x1, Pallas kernels: 114 us -> 108 us  [on_device(): pl.pallas_call(functools.partial(kernel, ring, groups, rows * ring, cols...]
where the time goes in v2:
time: 110 us
  Pallas kernels  108 us (98%)
  local copies, waits for them, and re-layouts  1.87 us (2%)
    pallas_call x1, Pallas kernels, on_device(): pl.pallas_call(functools.partial(kernel, ring, groups, rows * ring, cols...  108 us

profile of v2, /device:TPU:0, one launch (start us, length us, event | category | flops | bytes accessed | tf_op | source)
XLA Modules:
  0.0 109.9 jit_solution(16625325741876510881)
XLA Ops:
  0.0 108.0 %shard_map.28 = f32[64,2048]{1,0:T(8,128)} custom-call(bf16[2048,1024]{1,0:T(8,128)(2,1)} %vec_hbm.1, bf16[64,2048]{1,0:T(8,128)(2,1)} %cen_hbm.1), custom_call_target="tpu_custom_call" | custom-call | tf_op jit(solution)/shard_map/pallas_call | solution.py:546
  108.0 1.9 %copy.4 = f32[64,2048]{1,0:T(8,128)} copy(f32[64,2048]{1,0:T(8,128)} %shard_map.28) | data formatting | bytes 1048576
